TPU v7x, 512 devices: a whole 4x8x8 slice. The times are simulated.
512 devices in a mesh: sec: 64 (over x, y, core), mp: 8 (over z).
Axes of the slice: x: 4, y: 8, z: 8, core: 2. Of those that a mesh axis runs over, the one named last changes fastest.
Arguments:
- inputs: bfloat16 [8192, 2048], P('sec'), may hold values from -6 to 6
- expert_w: bfloat16 [8, 2048, 1024], P('mp', 'sec'), may hold values from -0.125 to 0.125
- gate_w: bfloat16 [2048, 6, 8], replicated, may hold values from -0.125 to 0.125
- tower_up: bfloat16 [64, 1024, 4096], P('sec', None, 'mp'), as said below
- tower_out: bfloat16 [64, 4096], P('sec', 'mp'), as said below
- sections: int32 [64], replicated, may hold values from 0 to 5, as said below
- tasks: int32 [8192, 6], P('sec'), may hold values from 0 to 1, as said below
- labels: int32 [8192, 6], P('sec'), may hold values 0 or 1
Outputs:
- input_grad: bfloat16 [8192, 2048], P('sec', 'mp')
Inputs may be any that keep to these rules, and one draw needn't show every extreme that they name: `sections`: each task owns one run of consecutive indices, the runs in task order, every task at least one index. `tasks`: in each aligned block of 128 examples, task t has at most 4 times as many examples as its section has indices of sec; every task reaches this bound in some block. `tower_up`: all indices of one section hold equal copies. `tower_out`: all indices of one section hold equal copies.
All inputs are finite; a program needn't handle non-finite values. No bound on the sum of `labels` on one device may be relied on, other than what follows from the above.
Results may differ from a plain program's by a relative error of at most 0.024.
Values may be sent and summed in bfloat16 or wider, within the bound.
No kernel may reach another device: no remote copies, remote signals or barrier semaphores. Data moves between devices by JAX's collectives and lax.ppermute only.
A program may use at most 64 MiB of HBM per device.

v0:
```python
import jax
import jax.numpy as jnp
from jax import lax
from jax.sharding import PartitionSpec as P

loss_scale = 64.0


def silu_slope(value, sig):
    return sig * (1.0 + value * (1.0 - sig))


def per_device(inputs, expert_w, gate_w, tower_up, tower_out, sections, tasks, labels):
    rows = inputs.shape[0]
    task_count = tasks.shape[1]
    n_sec = lax.axis_size("sec")
    pair_slots = 2 * rows // n_sec
    slots = n_sec * pair_slots
    local_w = expert_w[0]
    width = local_w.shape[1]
    picker = (jnp.arange(gate_w.shape[2], dtype=jnp.int32) == lax.axis_index("mp")).astype(
        jnp.float32
    )
    gate_logit = jnp.einsum("nd,dtk->ntk", inputs, gate_w, preferred_element_type=jnp.float32)
    raised = jnp.exp(gate_logit)
    gates = raised / jnp.sum(raised, axis=2, keepdims=True)
    mine = jnp.sum(gates * picker, axis=2)
    whole_w = lax.all_gather(local_w, "sec", axis=0, tiled=True)
    pre = jnp.dot(inputs, whole_w, preferred_element_type=jnp.float32)
    sig_pre = jax.nn.sigmoid(pre)
    expert_out = (pre * sig_pre).astype(jnp.bfloat16)
    task_ids = jnp.arange(task_count, dtype=jnp.int32)
    members = jnp.sum((sections[None, :] == task_ids[:, None]).astype(jnp.int32), axis=1)
    first = jnp.sum((sections[None, :] < task_ids[:, None]).astype(jnp.int32), axis=1)
    ranks = jnp.cumsum(tasks, axis=0) - tasks
    target = first[None, :] + ranks % members[None, :]
    place = target * pair_slots + ranks // members[None, :]
    place = jnp.where(tasks > 0, place, slots)
    pair_total = rows * task_count
    pair_ids = jnp.arange(pair_total, dtype=jnp.int32)
    source = (
        jnp.full((slots,), pair_total, jnp.int32).at[place.reshape(-1)].set(pair_ids, mode="drop")
    )
    filled = (source < pair_total).astype(jnp.float32)
    source = jnp.minimum(source, pair_total - 1)
    src_row = source // task_count
    src_task = source % task_count
    weight = mine[src_row, src_task] * filled
    contrib = weight[:, None] * expert_out[src_row].astype(jnp.float32)
    tag_out = (filled * (1.0 + labels[src_row, src_task].astype(jnp.float32))).astype(jnp.bfloat16)
    sent = lax.psum(contrib.astype(jnp.bfloat16), "mp")
    arrived, tag_in = (
        lax.all_to_all(
            sent.reshape(n_sec, pair_slots, -1), "sec", split_axis=0, concat_axis=0, tiled=True
        ),
        lax.all_to_all(
            tag_out.reshape(n_sec, pair_slots), "sec", split_axis=0, concat_axis=0, tiled=True
        ),
    )
    arrived = arrived.reshape(slots, -1)
    up_local = tower_up[0]
    out_local = tower_out[0].astype(jnp.float32)
    act = jnp.dot(arrived, up_local, preferred_element_type=jnp.float32)
    sig_act = jax.nn.sigmoid(act)
    partial_logit = jnp.sum(act * sig_act * out_local[None, :], axis=1)
    logit = lax.psum(partial_logit, "mp")
    tag_value = tag_in.reshape(slots).astype(jnp.float32)
    alive = (tag_value > 0.5).astype(jnp.float32)
    label_value = jnp.maximum(tag_value - 1.0, 0.0)
    slope = loss_scale * (jax.nn.sigmoid(logit) - label_value) * alive
    act_grad = (slope[:, None] * out_local[None, :] * silu_slope(act, sig_act)).astype(jnp.bfloat16)
    back = lax.dot_general(
        act_grad, up_local, (((1,), (1,)), ((), ())), preferred_element_type=jnp.float32
    )
    grads = lax.psum(back.astype(jnp.bfloat16), "mp")
    returned = lax.all_to_all(
        grads.reshape(n_sec, pair_slots, -1), "sec", split_axis=0, concat_axis=0, tiled=True
    ).reshape(slots, -1)
    padded = jnp.concatenate([returned, jnp.zeros((1, width), jnp.bfloat16)], axis=0)
    mixture_grad = padded[place]
    expert_grad = jnp.zeros((rows, width), jnp.float32)
    for task in range(task_count):
        expert_grad = expert_grad + mine[:, task : task + 1] * mixture_grad[:, task].astype(
            jnp.float32
        )
    gate_grad = jnp.einsum(
        "nte,ne->nt", mixture_grad, expert_out, preferred_element_type=jnp.float32
    )
    spread_sum = lax.psum(mine * gate_grad, "mp")
    gate_logit_grad = mine * (gate_grad - spread_sum)
    pre_grad = (expert_grad * silu_slope(pre, sig_pre)).astype(jnp.bfloat16)
    gate_cols = jnp.sum(gate_w.astype(jnp.float32) * picker, axis=2)
    gate_part = jnp.dot(gate_logit_grad, gate_cols.T, precision=lax.Precision.HIGHEST)
    input_part = lax.dot_general(
        pre_grad, whole_w, (((1,), (1,)), ((), ())), preferred_element_type=jnp.float32
    )
    return lax.psum_scatter(
        (input_part + gate_part).astype(jnp.bfloat16), "mp", scatter_dimension=1, tiled=True
    )


def solution(mesh):
    in_specs = (
        P("sec", None),
        P("mp", "sec", None),
        P(),
        P("sec", None, "mp"),
        P("sec", "mp"),
        P(),
        P("sec", None),
        P("sec", None),
    )
    out_specs = P("sec", "mp")
    return jax.shard_map(
        per_device, mesh=mesh, in_specs=in_specs, out_specs=out_specs, check_vma=False
    )
```

profile of v0, /device:TPU:2, one launch (start us, length us, event | category | flops | bytes accessed | tf_op | source)
XLA Modules:
  0.0 409.1 jit_solution(17913889090033370645)
XLA Ops:
  6.5 0.7 all-gather.3.cloned.1.call-update
  7.3 0.8 copy.35
  8.1 0.7 broadcast_compare_fusion
  8.8 0.1 copy.37
  8.9 0.2 reduce_window_sum.11
  9.1 0.8 convert_reduce_fusion.1
  9.9 1.3 compare_select_fusion
  11.3 0.1 reshape.93
  11.4 3.4 scatter_custom_fusion
  14.8 1.4 fusion.54
  16.3 1.4 gather_fusion.1
  17.6 1.4 gather_fusion
  19.1 79.5 %all-gather.3.cloned.1.call-done = bf16[1,2048,1024]{2,1,0:T(8,128)(2,1)} async-done(((bf16[1,32,1024]{2,1,0:T(8,128)(2,1)}), bf16[1,2048,1024]{2,1,0:T(8,128)(2,1)}) %all-gather.3.cloned.1.call-update) | async-done | bytes 4194320 | tf_op jit(solution)/shard_map/all_gather | solution.py:28
  98.6 3.8 multiply_convert_fusion.2
  102.4 1.2 gather_fusion.2
  103.5 0.2 multiply_convert_fusion
  103.7 1.0 reshape.94
  104.7 0.1 all_to_all.16
  104.9 16.0 %all_to_all.20 = bf16[64,1,4]{2,1,0:T(2,128)(2,1)S(1)} all-to-all(bf16[64,1,4]{2,1,0:T(2,128)(2,1)S(1)} %all_to_all.16), channel_id=1, replica_groups=mesh['sec'=64,'mp'=8] {'sec'}, dimensions={0} | all-to-all | bytes 1024 | tf_op jit(solution)/shard_map/all_to_all | solution.py:56
  120.8 62.6 %all-reduce.4.cloned.1.call-done = bf16[64,4,1024]{2,1,0:T(4,128)(2,1)} async-done(((bf16[64,4,1024]{2,1,0:T(4,128)(2,1)}), bf16[64,4,1024]{2,1,0:T(4,128)(2,1)}) %all-reduce.4.cloned.1.call-update) | async-done | bytes 524304 | tf_op jit(solution)/shard_map/psum | solution.py:51
  183.4 10.3 %all-to-all-start.1 = ((bf16[64,4,1024]{2,1,0:T(4,128)(2,1)}), bf16[64,4,1024]{2,1,0:T(4,128)(2,1)S(1)}, u32[]{:S(2)}, u32[]{:S(2)}) async-start(bf16[64,4,1024]{2,1,0:T(4,128)(2,1)} %all-reduce.4.cloned.1.call-done), calls=%async_computation.1 | async-start | bytes 1048576 | tf_op jit(solution)/shard_map/all_to_all | solution.py:53
  193.8 0.1 maximum_reduce_fusion
  193.9 0.1 max.8
  194.0 0.1 compare_reduce_fusion
  194.1 0.1 gt.15
  194.3 16.1 %all-to-all-done.1 = bf16[64,4,1024]{2,1,0:T(4,128)(2,1)S(1)} async-done(((bf16[64,4,1024]{2,1,0:T(4,128)(2,1)}), bf16[64,4,1024]{2,1,0:T(4,128)(2,1)S(1)}, u32[]{:S(2)}, u32[]{:S(2)}) %all-to-all-start.1) | async-done | bytes 524320 | tf_op jit(solution)/shard_map/all_to_all | solution.py:53
  210.4 0.1 reshape.95
  210.5 0.6 multiply_reduce_fusion
  211.1 16.3 %psum.29 = f32[256]{0:T(256)S(1)} all-reduce(f32[256]{0:T(256)S(1)} %get-tuple-element.29), channel_id=1, replica_groups=mesh['sec'=64,'mp'=8] {'mp'}, use_global_device_ids=true, to_apply=%region_8.9 | all-reduce | flops 256 | bytes 2048 | tf_op jit(solution)/shard_map/psum | solution.py:66
  227.4 0.7 convolution_convert_fusion
  228.1 1.0 reshape.96
  229.1 75.2 %all-reduce.6.cloned.1.call-done = bf16[64,4,1024]{2,1,0:T(4,128)(2,1)} async-done(((bf16[64,4,1024]{2,1,0:T(4,128)(2,1)}), bf16[64,4,1024]{2,1,0:T(4,128)(2,1)}) %all-reduce.6.cloned.1.call-update) | async-done | bytes 524304 | tf_op jit(solution)/shard_map/psum | solution.py:75
  304.4 10.3 %all-to-all-start.2 = ((bf16[64,4,1024]{2,1,0:T(4,128)(2,1)}), bf16[64,4,1024]{2,1,0:T(4,128)(2,1)S(1)}, u32[]{:S(2)}, u32[]{:S(2)}) async-start(bf16[64,4,1024]{2,1,0:T(4,128)(2,1)} %all-reduce.6.cloned.1.call-done), calls=%async_computation.2 | async-start | bytes 1048576 | tf_op jit(solution)/shard_map/all_to_all | solution.py:76
  314.6 0.2 reduce-scatter.2.cloned.1.call-start
  314.9 0.1 reshape.127
  315.0 0.2 multiply_reduce_fusion.1
  315.2 0.5 slice_bitcast_fusion.5
  315.8 15.5 %all-to-all-done.2 = bf16[64,4,1024]{2,1,0:T(4,128)(2,1)S(1)} async-done(((bf16[64,4,1024]{2,1,0:T(4,128)(2,1)}), bf16[64,4,1024]{2,1,0:T(4,128)(2,1)S(1)}, u32[]{:S(2)}, u32[]{:S(2)}) %all-to-all-start.2) | async-done | bytes 524320 | tf_op jit(solution)/shard_map/all_to_all | solution.py:76
  331.3 0.1 reshape.97
  331.5 3.6 gather_fusion.3
  335.0 2.5 reshape.126
  337.5 3.7 fusion.53
  341.3 1.3 fusion.24
  342.6 0.1 copy.46
  342.7 16.3 %psum.31 = f32[128,6]{0,1:T(8,128)S(1)} all-reduce(f32[128,6]{0,1:T(8,128)S(1)} %bitcast_multiply_fusion), channel_id=1, replica_groups=mesh['sec'=64,'mp'=8] {'mp'}, use_global_device_ids=true, to_apply=%region_10.11 | all-reduce | flops 768 | bytes 6144 | tf_op jit(solution)/shard_map/psum | solution.py:89
  358.9 1.0 fusion.45
  360.0 6.1 %fusion.8 = bf16[128,2048]{1,0:T(8,128)(2,1)} fusion(f32[128,2048]{1,0:T(8,128)S(1)} %fusion.45, bf16[1,2048,1024]{2,1,0:T(8,128)(2,1)} %all-gather.3.cloned.1.call-done, f32[128,1024]{1,0:T(8,128)} %get-tuple-element.28, bf16[128,1,1024]{2,1,0:T(2,128)(2,1)} %get-tuple-element.16, bf16[128,1,1024]{2,1,0:T(2,128)(2,1)} %get-tuple-element.12, ...), kind=kOutput, calls=%fused_computation.11 | convolution fusion | flops 540803072 | bytes 7867392 | tf_op jit(solution)/shard_map/dot_general | solution.py:94
  366.1 36.4 %reduce-scatter.2.cloned.1.call-done = bf16[128,256]{1,0:T(8,128)(2,1)} async-done(((bf16[128,2048]{1,0:T(8,128)(2,1)}), bf16[128,256]{1,0:T(8,128)(2,1)}) %reduce-scatter.2.cloned.1.call-update) | async-done | bytes 65552 | tf_op jit(solution)/shard_map/reduce_scatter | solution.py:97
  (29 shorter events, 0.3 us)
Async XLA Ops:
  6.5 204.0 %copy-start = (bf16[1,1024,512]{2,1,0:T(8,128)(2,1)S(1)}, bf16[1,1024,512]{2,1,0:T(8,128)(2,1)}, u32[]{:S(2)}) copy-start(bf16[1,1024,512]{2,1,0:T(8,128)(2,1)} %param.11) | copy-start | bytes 3145732
  6.5 92.1 %copy-start.4 = (bf16[128,2048]{1,0:T(8,128)(2,1)S(1)}, bf16[128,2048]{1,0:T(8,128)(2,1)}, u32[]{:S(2)}) copy-start(bf16[128,2048]{1,0:T(8,128)(2,1)} %param.8) | copy-start | bytes 1572868
  6.5 11.1 %copy-start.1 = (s32[128,6]{0,1:T(8,128)S(1)}, s32[128,6]{0,1:T(8,128)}, u32[]{:S(2)}) copy-start(s32[128,6]{0,1:T(8,128)} %param.15) | copy-start | bytes 9220
  6.5 92.0 %all-gather.3.cloned.1.call-start = ((), (), s32[]{:S(2)}) async-start(), calls=%async_computation.7 | async-start | bytes 4259840 | tf_op jit(solution)/shard_map/all_gather | solution.py:28
  7.3 176.2 %all-reduce.4.cloned.1.call-start = ((), (), s32[]{:S(2)}) async-start(), calls=%async_computation.4 | async-start | bytes 1048576 | tf_op jit(solution)/shard_map/psum | solution.py:51
  103.5 90.3 %copy-start.3 = (bf16[1,512]{1,0:T(2,128)(2,1)S(1)}, bf16[1,512]{1,0:T(2,128)(2,1)}, u32[]{:S(2)}) copy-start(bf16[1,512]{1,0:T(2,128)(2,1)} %param.12) | copy-start | bytes 3076
  183.4 26.9 %all-to-all-start.1 = ((bf16[64,4,1024]{2,1,0:T(4,128)(2,1)}), bf16[64,4,1024]{2,1,0:T(4,128)(2,1)S(1)}, u32[]{:S(2)}, u32[]{:S(2)}) async-start(bf16[64,4,1024]{2,1,0:T(4,128)(2,1)} %all-reduce.4.cloned.1.call-done), calls=%async_computation.1 | async-start | bytes 1048576 | tf_op jit(solution)/shard_map/all_to_all | solution.py:53
  193.7 110.6 %all-reduce.6.cloned.1.call-start = ((), (), s32[]{:S(2)}) async-start(), calls=%async_computation.5 | async-start | bytes 1048576 | tf_op jit(solution)/shard_map/psum | solution.py:75
  228.1 87.0 %copy-start.2 = (bf16[2048,6,8]{0,2,1:T(8,128)(2,1)S(1)}, bf16[2048,6,8]{0,2,1:T(8,128)(2,1)}, u32[]{:S(2)}) copy-start(bf16[2048,6,8]{0,2,1:T(8,128)(2,1)} %param.10) | copy-start | bytes 589828
  304.4 26.9 %all-to-all-start.2 = ((bf16[64,4,1024]{2,1,0:T(4,128)(2,1)}), bf16[64,4,1024]{2,1,0:T(4,128)(2,1)S(1)}, u32[]{:S(2)}, u32[]{:S(2)}) async-start(bf16[64,4,1024]{2,1,0:T(4,128)(2,1)} %all-reduce.6.cloned.1.call-done), calls=%async_computation.2 | async-start | bytes 1048576 | tf_op jit(solution)/shard_map/all_to_all | solution.py:76
  314.6 87.9 %reduce-scatter.2.cloned.1.call-start = ((), (), s32[]{:S(2)}) async-start(), calls=%async_computation.6 | async-start | bytes 589824 | tf_op jit(solution)/shard_map/reduce_scatter | solution.py:97
Sparse Core Ops, SparseCore 0:
  10.7 87.8 all-gather.2
  104.9 78.5 all-reduce.3
  229.2 75.0 all-reduce.5
  366.2 36.2 reduce-scatter.1
where the time goes:
time: 410 us; the launch traced here: 409 us
  waiting for transfers between devices  286 us (70%)
  blocking collectives  48.5 us (12%)
  local copies, waits for them, and re-layouts  21.5 us (5%)
  starting transfers between devices  20.9 us (5%)
  matrix products  14.9 us (4%)
  between operations  13.4 us (3%)
    all_gather x1, waiting for transfers between devices, per_device(): whole_w = lax.all_gather(local_w, 'sec', axis=0, tiled=True)  79.5 us
    psum x1, waiting for transfers between devices, per_device(): grads = lax.psum(back.astype(jnp.bfloat16), 'mp')  75.2 us
    psum x1, waiting for transfers between devices, per_device(): sent = lax.psum(contrib.astype(jnp.bfloat16), 'mp')  62.6 us
    reduce_scatter x1, waiting for transfers between devices, per_device(): lax.psum_scatter((input_part + gate_part).astype(jnp.bfloat16), 'mp', sca...  36.4 us
    psum x1, blocking collectives, per_device(): logit = lax.psum(partial_logit, 'mp')  16.3 us
    psum x1, blocking collectives, per_device(): spread_sum = lax.psum(mine * gate_grad, 'mp')  16.3 us
    all_to_all x1, waiting for transfers between devices, per_device(): lax.all_to_all(sent.reshape(n_sec, pair_slots, -1), 'sec', split_axis=0,...  16.1 us
    all_to_all x1, blocking collectives, per_device(): lax.all_to_all(tag_out.reshape(n_sec, pair_slots), 'sec', split_axis=0, c...  16 us
  transfers between devices with their start and end apart: 6, of which 6 were waited for; matrix products, arithmetic and copies ran while one was open for 3% of the time, Pallas kernels for 0%

commit v1 on v0

--- a/solution.py
+++ b/solution.py
@@ -25,7 +25,9 @@
     raised = jnp.exp(gate_logit)
     gates = raised / jnp.sum(raised, axis=2, keepdims=True)
     mine = jnp.sum(gates * picker, axis=2)
-    whole_w = lax.all_gather(local_w, "sec", axis=0, tiled=True)
+    whole_w = jnp.concatenate(
+        lax.all_to_all(jnp.stack(lax.axis_size("sec") * [local_w], axis=0), "sec", 0, 0), 0
+    )
     pre = jnp.dot(inputs, whole_w, preferred_element_type=jnp.float32)
     sig_pre = jax.nn.sigmoid(pre)
     expert_out = (pre * sig_pre).astype(jnp.bfloat16)

time: 410 us -> 429 us (1.046)
  starting transfers between devices: 20.9 us -> 32 us
  waiting for transfers between devices: 286 us -> 295 us
    all_to_all x0 -> x1, waiting for transfers between devices: none -> 86 us  [per_device(): lax.all_to_all(jnp.stack(lax.axis_size('sec') * [local_w], axis=0), 'sec'...]
    all_gather x1 -> x0, waiting for transfers between devices: 79.5 us -> none  [per_device(): whole_w = lax.all_gather(local_w, 'sec', axis=0, tiled=True)]
    all_to_all x0 -> x1, starting transfers between devices: none -> 11.1 us  [per_device(): lax.all_to_all(jnp.stack(lax.axis_size('sec') * [local_w], axis=0), 'sec'...]
  transfers between devices with their start and end apart: 6 -> 6, of which waited for: 6 -> 6; matrix products, arithmetic and copies ran while one was open for 3% -> 2% of each run, Pallas kernels for 0% -> 0%
where the time goes in v1:
time: 429 us; the launch traced here: 428 us
  waiting for transfers between devices  295 us (69%)
  blocking collectives  47.8 us (11%)
  starting transfers between devices  32 us (7%)
  local copies, waits for them, and re-layouts  24.3 us (6%)
  matrix products  13.8 us (3%)
  between operations  13.4 us (3%)
    all_to_all x1, waiting for transfers between devices, per_device(): lax.all_to_all(jnp.stack(lax.axis_size('sec') * [local_w], axis=0), 'sec'...  86 us
    psum x1, waiting for transfers between devices, per_device(): grads = lax.psum(back.astype(jnp.bfloat16), 'mp')  75.2 us
    psum x1, waiting for transfers between devices, per_device(): sent = lax.psum(contrib.astype(jnp.bfloat16), 'mp')  65.4 us
    reduce_scatter x1, waiting for transfers between devices, per_device(): lax.psum_scatter((input_part + gate_part).astype(jnp.bfloat16), 'mp', sca...  36.4 us
    psum x1, blocking collectives, per_device(): spread_sum = lax.psum(mine * gate_grad, 'mp')  16.3 us
    psum x1, blocking collectives, per_device(): logit = lax.psum(partial_logit, 'mp')  16.2 us
    all_to_all x1, waiting for transfers between devices, per_device(): lax.all_to_all(sent.reshape(n_sec, pair_slots, -1), 'sec', split_axis=0,...  16.1 us
    all_to_all x1, waiting for transfers between devices, per_device(): lax.all_to_all(grads.reshape(n_sec, pair_slots, -1), 'sec', split_axis=0,...  15.5 us
  transfers between devices with their start and end apart: 6, of which 6 were waited for; matrix products, arithmetic and copies ran while one was open for 2% of the time, Pallas kernels for 0%

profile of v1, /device:TPU:2, one launch (start us, length us, event | category | flops | bytes accessed | tf_op | source)
XLA Modules:
  0.0 428.4 jit_solution(2151596215609290752)
XLA Ops:
  6.5 3.4 stack.3
  10.0 11.1 %all-to-all-start.1 = ((bf16[64,32,1024]{2,1,0:T(8,128)(2,1)}), bf16[64,32,1024]{2,1,0:T(8,128)(2,1)}, u32[]{:S(2)}, u32[]{:S(2)}) async-start(bf16[64,32,1024]{2,1,0:T(8,128)(2,1)} %stack.3), calls=%async_computation.1 | async-start | bytes 8388608 | tf_op jit(solution)/shard_map/all_to_all | solution.py:29
  21.2 0.1 copy.35
  21.3 0.1 copy.37
  21.5 0.2 reduce_window_sum.11
  21.6 0.1 convert_reduce_fusion.1
  21.8 1.3 compare_select_fusion
  23.1 0.1 reshape.97
  23.3 3.4 scatter_custom_fusion
  26.7 0.3 fusion.45
  27.1 1.4 gather_fusion.1
  28.5 1.4 gather_fusion
  29.9 86.0 %all-to-all-done.1 = bf16[64,32,1024]{2,1,0:T(8,128)(2,1)} async-done(((bf16[64,32,1024]{2,1,0:T(8,128)(2,1)}), bf16[64,32,1024]{2,1,0:T(8,128)(2,1)}, u32[]{:S(2)}, u32[]{:S(2)}) %all-to-all-start.1) | async-done | bytes 4194336 | tf_op jit(solution)/shard_map/all_to_all | solution.py:29
  115.9 3.8 multiply_convert_fusion.2
  119.7 1.2 gather_fusion.2
  120.8 0.2 multiply_convert_fusion
  121.0 1.0 reshape.99
  122.0 0.1 all_to_all.20
  122.2 15.3 %all_to_all.25 = bf16[64,1,4]{2,1,0:T(2,128)(2,1)S(1)} all-to-all(bf16[64,1,4]{2,1,0:T(2,128)(2,1)S(1)} %all_to_all.20), channel_id=1, replica_groups=mesh['sec'=64,'mp'=8] {'sec'}, dimensions={0} | all-to-all | bytes 1024 | tf_op jit(solution)/shard_map/all_to_all | solution.py:58
  137.4 65.4 %all-reduce.4.cloned.1.call-done = bf16[64,4,1024]{2,1,0:T(4,128)(2,1)} async-done(((bf16[64,4,1024]{2,1,0:T(4,128)(2,1)}), bf16[64,4,1024]{2,1,0:T(4,128)(2,1)}) %all-reduce.4.cloned.1.call-update) | async-done | bytes 524304 | tf_op jit(solution)/shard_map/psum | solution.py:53
  202.9 10.3 %all-to-all-start.2 = ((bf16[64,4,1024]{2,1,0:T(4,128)(2,1)}), bf16[64,4,1024]{2,1,0:T(4,128)(2,1)S(1)}, u32[]{:S(2)}, u32[]{:S(2)}) async-start(bf16[64,4,1024]{2,1,0:T(4,128)(2,1)} %all-reduce.4.cloned.1.call-done), calls=%async_computation.2 | async-start | bytes 1048576 | tf_op jit(solution)/shard_map/all_to_all | solution.py:55
  213.2 0.1 maximum_reduce_fusion
  213.3 0.1 max.8
  213.4 0.1 compare_reduce_fusion
  213.5 0.1 gt.15
  213.7 16.1 %all-to-all-done.2 = bf16[64,4,1024]{2,1,0:T(4,128)(2,1)S(1)} async-done(((bf16[64,4,1024]{2,1,0:T(4,128)(2,1)}), bf16[64,4,1024]{2,1,0:T(4,128)(2,1)S(1)}, u32[]{:S(2)}, u32[]{:S(2)}) %all-to-all-start.2) | async-done | bytes 524320 | tf_op jit(solution)/shard_map/all_to_all | solution.py:55
  229.8 0.1 reshape.100
  229.9 0.6 multiply_reduce_fusion
  230.6 16.2 %psum.29 = f32[256]{0:T(256)S(1)} all-reduce(f32[256]{0:T(256)S(1)} %get-tuple-element.29), channel_id=1, replica_groups=mesh['sec'=64,'mp'=8] {'mp'}, use_global_device_ids=true, to_apply=%region_8.9 | all-reduce | flops 256 | bytes 2048 | tf_op jit(solution)/shard_map/psum | solution.py:68
  246.8 0.6 convolution_convert_fusion
  247.4 1.0 reshape.101
  248.5 75.2 %all-reduce.6.cloned.1.call-done = bf16[64,4,1024]{2,1,0:T(4,128)(2,1)} async-done(((bf16[64,4,1024]{2,1,0:T(4,128)(2,1)}), bf16[64,4,1024]{2,1,0:T(4,128)(2,1)}) %all-reduce.6.cloned.1.call-update) | async-done | bytes 524304 | tf_op jit(solution)/shard_map/psum | solution.py:77
  323.7 10.3 %all-to-all-start.3 = ((bf16[64,4,1024]{2,1,0:T(4,128)(2,1)}), bf16[64,4,1024]{2,1,0:T(4,128)(2,1)S(1)}, u32[]{:S(2)}, u32[]{:S(2)}) async-start(bf16[64,4,1024]{2,1,0:T(4,128)(2,1)} %all-reduce.6.cloned.1.call-done), calls=%async_computation.3 | async-start | bytes 1048576 | tf_op jit(solution)/shard_map/all_to_all | solution.py:78
  333.9 0.2 reduce-scatter.2.cloned.1.call-start
  334.2 0.1 reshape.132
  334.3 0.2 multiply_reduce_fusion.1
  334.5 0.6 slice_bitcast_fusion.5
  335.1 15.5 %all-to-all-done.3 = bf16[64,4,1024]{2,1,0:T(4,128)(2,1)S(1)} async-done(((bf16[64,4,1024]{2,1,0:T(4,128)(2,1)}), bf16[64,4,1024]{2,1,0:T(4,128)(2,1)S(1)}, u32[]{:S(2)}, u32[]{:S(2)}) %all-to-all-start.3) | async-done | bytes 524320 | tf_op jit(solution)/shard_map/all_to_all | solution.py:78
  350.6 0.1 reshape.102
  350.8 3.6 gather_fusion.3
  354.4 2.5 reshape.131
  356.8 3.7 fusion.44
  360.6 1.3 fusion.15
  361.9 0.1 copy.46
  362.0 16.3 %psum.31 = f32[128,6]{0,1:T(8,128)S(1)} all-reduce(f32[128,6]{0,1:T(8,128)S(1)} %bitcast_multiply_fusion), channel_id=1, replica_groups=mesh['sec'=64,'mp'=8] {'mp'}, use_global_device_ids=true, to_apply=%region_10.11 | all-reduce | flops 768 | bytes 6144 | tf_op jit(solution)/shard_map/psum | solution.py:91
  378.2 5.3 %fusion.17 = f32[128,2048]{1,0:T(8,128)S(1)} fusion(bf16[2048,1024]{1,0:T(8,128)(2,1)} %bitcast.4, f32[128,1024]{1,0:T(8,128)} %get-tuple-element.28, bf16[128,1,1024]{2,1,0:T(2,128)(2,1)} %get-tuple-element.16, bf16[128,1,1024]{2,1,0:T(2,128)(2,1)} %get-tuple-element.12, bf16[128,1,1024]{2,1,0:T(2,128)(2,1)} %get-tuple-element.13, ...), kind=kOutput, calls=%fused_computation.38 | convolution fusion | flops 540278784 | bytes 7343104 | tf_op jit(solution)/shard_map/dot_general | solution.py:96
  383.5 1.9 fusion.1
  385.4 36.4 %reduce-scatter.2.cloned.1.call-done = bf16[128,256]{1,0:T(8,128)(2,1)} async-done(((bf16[128,2048]{1,0:T(8,128)(2,1)}), bf16[128,256]{1,0:T(8,128)(2,1)}) %reduce-scatter.2.cloned.1.call-update) | async-done | bytes 65552 | tf_op jit(solution)/shard_map/reduce_scatter | solution.py:99
  (33 shorter events, 0.3 us)
Async XLA Ops:
  6.5 223.4 %copy-start = (bf16[1,1024,512]{2,1,0:T(8,128)(2,1)S(1)}, bf16[1,1024,512]{2,1,0:T(8,128)(2,1)}, u32[]{:S(2)}) copy-start(bf16[1,1024,512]{2,1,0:T(8,128)(2,1)} %param.11) | copy-start | bytes 3145732
  10.0 11.2 %copy-start.3 = (s32[128,6]{0,1:T(8,128)S(1)}, s32[128,6]{0,1:T(8,128)}, u32[]{:S(2)}) copy-start(s32[128,6]{0,1:T(8,128)} %param.14) | copy-start | bytes 9220
  10.0 11.7 %copy-start.6 = (s32[64]{0:T(128)S(1)}, s32[64]{0:T(128)}, u32[]{:S(2)}) copy-start(s32[64]{0:T(128)} %param.13) | copy-start | bytes 772
  10.0 16.7 %copy-start.2 = (bf16[2048,6,8]{0,2,1:T(8,128)(2,1)S(1)}, bf16[2048,6,8]{0,2,1:T(8,128)(2,1)}, u32[]{:S(2)}) copy-start(bf16[2048,6,8]{0,2,1:T(8,128)(2,1)} %param.10) | copy-start | bytes 589828
  10.0 16.7 %copy-start.5 = (bf16[128,2048]{1,0:T(8,128)(2,1)S(1)}, bf16[128,2048]{1,0:T(8,128)(2,1)}, u32[]{:S(2)}) copy-start(bf16[128,2048]{1,0:T(8,128)(2,1)} %param.8) | copy-start | bytes 1572868
  10.0 105.9 %all-to-all-start.1 = ((bf16[64,32,1024]{2,1,0:T(8,128)(2,1)}), bf16[64,32,1024]{2,1,0:T(8,128)(2,1)}, u32[]{:S(2)}, u32[]{:S(2)}) async-start(bf16[64,32,1024]{2,1,0:T(8,128)(2,1)} %stack.3), calls=%async_computation.1 | async-start | bytes 8388608 | tf_op jit(solution)/shard_map/all_to_all | solution.py:29
  21.1 7.3 %copy-start.1 = (s32[128,6]{0,1:T(8,128)S(1)}, s32[128,6]{0,1:T(8,128)}, u32[]{:S(2)}) copy-start(s32[128,6]{0,1:T(8,128)} %param.15) | copy-start | bytes 9220
  21.1 181.7 %all-reduce.4.cloned.1.call-start = ((), (), s32[]{:S(2)}) async-start(), calls=%async_computation.5 | async-start | bytes 1048576 | tf_op jit(solution)/shard_map/psum | solution.py:53
  120.8 92.4 %copy-start.4 = (bf16[1,512]{1,0:T(2,128)(2,1)S(1)}, bf16[1,512]{1,0:T(2,128)(2,1)}, u32[]{:S(2)}) copy-start(bf16[1,512]{1,0:T(2,128)(2,1)} %param.12) | copy-start | bytes 3076
  202.9 26.9 %all-to-all-start.2 = ((bf16[64,4,1024]{2,1,0:T(4,128)(2,1)}), bf16[64,4,1024]{2,1,0:T(4,128)(2,1)S(1)}, u32[]{:S(2)}, u32[]{:S(2)}) async-start(bf16[64,4,1024]{2,1,0:T(4,128)(2,1)} %all-reduce.4.cloned.1.call-done), calls=%async_computation.2 | async-start | bytes 1048576 | tf_op jit(solution)/shard_map/all_to_all | solution.py:55
  213.1 110.5 %all-reduce.6.cloned.1.call-start = ((), (), s32[]{:S(2)}) async-start(), calls=%async_computation.6 | async-start | bytes 1048576 | tf_op jit(solution)/shard_map/psum | solution.py:77
  323.7 26.9 %all-to-all-start.3 = ((bf16[64,4,1024]{2,1,0:T(4,128)(2,1)}), bf16[64,4,1024]{2,1,0:T(4,128)(2,1)S(1)}, u32[]{:S(2)}, u32[]{:S(2)}) async-start(bf16[64,4,1024]{2,1,0:T(4,128)(2,1)} %all-reduce.6.cloned.1.call-done), calls=%async_computation.3 | async-start | bytes 1048576 | tf_op jit(solution)/shard_map/all_to_all | solution.py:78
  333.9 87.9 %reduce-scatter.2.cloned.1.call-start = ((), (), s32[]{:S(2)}) async-start(), calls=%async_computation.7 | async-start | bytes 589824 | tf_op jit(solution)/shard_map/reduce_scatter | solution.py:99
Sparse Core Ops, SparseCore 0:
  122.2 80.6 all-reduce.3
  248.6 75.0 all-reduce.5
  385.5 36.2 reduce-scatter.1
